TPU v7x, 32 devices: a whole 2x2x4 slice. The times are simulated.
32 devices in a mesh: vocab: 8 (over z, x), dp: 4 (over y, core).
Axes of the slice: x: 2, y: 2, z: 4, core: 2. Of those that a mesh axis runs over, the one named last changes fastest.
Arguments:
- teacher_hidden: bfloat16 [512, 5376], P('dp'), may hold values from -48 to 48
- student_hidden: bfloat16 [512, 2560], P('dp'), may hold values from -48 to 48
- teacher_codes: bfloat16 [16384, 5376], P(('vocab', 'dp')), may hold values from -8 to 7, as said below
- teacher_scales: float32 [16384, 42], P(('vocab', 'dp')), may hold values from 0.003 to 0.07
- student_weight: bfloat16 [16384, 2560], P(('vocab', 'dp')), may hold values from -1 to 1
- loss_scale: bfloat16 [512], P('dp'), may hold values from 2 to 20
Outputs:
- kl: float32 [512], P('dp')
- grad_hidden: bfloat16 [512, 2560], P('dp', 'vocab')
- grad_weight: bfloat16 [16384, 2560], P(('vocab', 'dp'))
Inputs may be any that keep to these rules, and one draw needn't show every extreme that they name: `teacher_codes`: whole numbers.
All inputs are finite; a program needn't handle non-finite values.
Results may differ from a plain program's by a relative error of at most 0.0085.
Values may be sent and summed in bfloat16 or wider, within the bound.
A program may use at most 128 MiB of HBM per device.

v0:
```python
import jax
import jax.numpy as jnp
from jax import lax
from jax.sharding import PartitionSpec as P

GROUP = 128


def dequantize(code_values, scales):
    row_count = code_values.shape[0]
    grouped = code_values.astype(jnp.float32).reshape(row_count, -1, GROUP) * scales[:, :, None]
    return grouped.reshape(row_count, -1).astype(jnp.bfloat16)


def contract_last(left_rows, right_rows):
    return lax.dot_general(
        left_rows, right_rows, (((1,), (1,)), ((), ())), preferred_element_type=jnp.float32
    )


def local(
    teacher_hidden, student_hidden, teacher_codes, teacher_scales, student_weight, loss_scale
):
    tok_rows = teacher_hidden.shape[0]
    teacher_all, student_all, scale_all = (
        lax.all_gather(teacher_hidden, "dp", axis=0, tiled=True),
        lax.all_gather(student_hidden, "dp", axis=0, tiled=True),
        lax.all_gather(loss_scale, "dp", axis=0, tiled=True),
    )
    teacher_table = dequantize(teacher_codes, teacher_scales)
    teacher_logits = contract_last(teacher_all, teacher_table)
    student_logits = contract_last(student_all, student_weight)
    teacher_local = jnp.max(teacher_logits, axis=1)
    student_local = jnp.max(student_logits, axis=1)
    teacher_top, student_top = lax.pmax((teacher_local, student_local), ("vocab", "dp"))
    teacher_exp = jnp.exp(teacher_logits - teacher_top[:, None])
    student_exp = jnp.exp(student_logits - student_top[:, None])
    teacher_total, cross_total, student_total = lax.psum(
        (
            jnp.sum(teacher_exp, axis=1),
            jnp.sum(teacher_exp * (teacher_logits - student_logits), axis=1),
            jnp.sum(student_exp, axis=1),
        ),
        ("vocab", "dp"),
    )
    teacher_lse = teacher_top + jnp.log(teacher_total)
    student_lse = student_top + jnp.log(student_total)
    divergence = cross_total / teacher_total - teacher_lse + student_lse
    own_start = lax.axis_index("dp") * tok_rows
    kl = lax.dynamic_slice_in_dim(divergence, own_start, tok_rows, 0)
    teacher_prob = jnp.exp(teacher_logits - teacher_lse[:, None])
    student_prob = jnp.exp(student_logits - student_lse[:, None])
    logit_grad = (scale_all.astype(jnp.float32)[:, None] * (student_prob - teacher_prob)).astype(
        jnp.bfloat16
    )
    grad_weight = lax.dot_general(
        logit_grad, student_all, (((0,), (0,)), ((), ())), preferred_element_type=jnp.float32
    ).astype(jnp.bfloat16)
    token_part = lax.psum_scatter(
        jnp.dot(logit_grad, student_weight, preferred_element_type=jnp.float32),
        "dp",
        scatter_dimension=0,
        tiled=True,
    )
    grad_hidden = lax.psum_scatter(token_part, "vocab", scatter_dimension=1, tiled=True).astype(
        jnp.bfloat16
    )
    return (kl, grad_hidden, grad_weight)


def solution(mesh):
    in_specs = (
        P("dp", None),
        P("dp", None),
        P(("vocab", "dp"), None),
        P(("vocab", "dp"), None),
        P(("vocab", "dp"), None),
        P("dp"),
    )
    out_specs = (P("dp"), P("dp", "vocab"), P(("vocab", "dp"), None))
    return jax.shard_map(local, mesh=mesh, in_specs=in_specs, out_specs=out_specs, check_vma=False)
```

profile of v0, /device:TPU:0, one launch (start us, length us, event | category | flops | bytes accessed | tf_op | source)
XLA Modules:
  0.0 305.5 jit_solution(14762963266301238189)
XLA Ops:
  7.2 0.0 copy-start
  7.2 0.0 all-gather.6.cloned.1.call-start
  7.2 0.7 all-gather.6.cloned.1.call-update
  7.9 0.0 all-gather.4.cloned.1.call-start
  8.0 0.7 all-gather.4.cloned.1.call-update
  8.7 0.0 copy-start.2
  8.7 0.0 copy-start.1
  8.7 0.0 reduce-scatter.5.cloned.1.call-start
  8.7 8.3 %copy.13 = bf16[512,5376]{0,1:T(8,128)(2,1)} copy(bf16[512,5376]{1,0:T(8,128)(2,1)} %param.8) | data formatting | bytes 11010048 | tf_op args[2]
  17.0 0.0 copy-done.2
  17.0 6.0 %all-gather = bf16[4,1,128]{2,1,0:T(2,128)(2,1)S(1)} all-gather(bf16[1,1,128]{2,1,0:T(2,128)(2,1)S(1)} %bitcast.41), channel_id=1, replica_groups=mesh['vocab'=8,'dp'=4] {'dp'}, dimensions={0}, use_global_device_ids=true | all-gather | bytes 1280 | tf_op jit(solution)/shard_map/all_gather | solution.py:28
  23.0 0.0 copy-done.1
  23.0 6.1 %fusion = bf16[512,5376]{0,1:T(8,128)(2,1)} fusion(bf16[512,5376]{0,1:T(8,128)(2,1)} %copy.13, f32[512,42]{0,1:T(8,128)S(1)} %copy-done.1), kind=kLoop, calls=%fused_computation.1 | loop fusion | flops 8257536 | bytes 11096064 | tf_op jit(solution)/shard_map/convert_element_type | solution.py:12
  29.2 8.7 %all-gather.6.cloned.1.call-done = bf16[512,2560]{1,0:T(8,128)(2,1)} async-done(((bf16[128,2560]{1,0:T(8,128)(2,1)}), bf16[512,2560]{1,0:T(8,128)(2,1)}) %all-gather.6.cloned.1.call-update) | async-done | bytes 2621456 | tf_op jit(solution)/shard_map/all_gather | solution.py:27
  37.8 0.0 copy-done
  37.8 4.3 %fusion.9 = (f32[512]{0:T(512)S(1)}, f32[512,512]{0,1:T(8,128)}) fusion(bf16[512,2560]{1,0:T(8,128)(2,1)} %all-gather.6.cloned.1.call-done, bf16[512,2560]{1,0:T(8,128)(2,1)S(1)} %copy-done), kind=kOutput, calls=%fused_computation.18 | convolution fusion | flops 1342438912 | bytes 6293504 | tf_op jit(solution)/shard_map/dot_general | solution.py:16
  42.1 39.2 %all-gather.4.cloned.1.call-done = bf16[512,5376]{1,0:T(8,128)(2,1)} async-done(((bf16[128,5376]{1,0:T(8,128)(2,1)}), bf16[512,5376]{1,0:T(8,128)(2,1)}) %all-gather.4.cloned.1.call-update) | async-done | bytes 5505040 | tf_op jit(solution)/shard_map/all_gather | solution.py:26
  81.3 8.2 %fusion.10 = (f32[512]{0:T(512)S(1)}, f32[512,512]{1,0:T(8,128)}) fusion(bf16[512,5376]{0,1:T(8,128)(2,1)} %fusion, bf16[512,5376]{1,0:T(8,128)(2,1)} %all-gather.4.cloned.1.call-done), kind=kOutput, calls=%fused_computation.19 | convolution fusion | flops 2818833920 | bytes 12060672 | tf_op jit(solution)/shard_map/dot_general | solution.py:16
  89.6 39.2 %all-reduce.1 = (f32[512]{0:T(512)S(1)}, f32[512]{0:T(512)S(1)}) all-reduce(f32[512]{0:T(512)S(1)} %get-tuple-element.23, f32[512]{0:T(512)S(1)} %get-tuple-element.25), channel_id=1, replica_groups=mesh['vocab'=8,'dp'=4] {'vocab','dp'}, use_global_device_ids=true, to_apply=%region_7.0 | all-reduce | flops 1024 | bytes 8192 | tf_op jit(solution)/shard_map/pmax | solution.py:35
  128.8 1.9 fusion.3
  130.7 41.1 %all-reduce = (f32[512]{0:T(512)S(1)}, f32[512]{0:T(512)S(1)}, f32[512]{0:T(512)S(1)}) all-reduce(f32[512]{0:T(512)S(1)} %get-tuple-element.14, f32[512]{0:T(512)S(1)} %get-tuple-element.13, f32[512]{0:T(512)S(1)} %get-tuple-element.12), channel_id=1, replica_groups=mesh['vocab'=8,'dp'=4] {'vocab','dp'}, use_global_device_ids=true, to_apply=%region_9.0 | all-reduce | flops 1536 | bytes 12288 | tf_op jit(solution)/shard_map/psum | solution.py:38
  171.8 1.8 fusion.7
  173.7 3.9 %fusion.11 = f32[512,2560]{1,0:T(8,128)} fusion(bf16[512,512]{0,1:T(8,128)(2,1)S(1)} %fusion.7, bf16[512,2560]{1,0:T(8,128)(2,1)S(1)} %copy-done), kind=kOutput, calls=%fused_computation.20 | convolution fusion | flops 1342177280 | bytes 8388608 | tf_op jit(solution)/shard_map/dot_general | solution.py:60
  177.5 0.0 reduce-scatter.5.cloned.1.call-update
  177.6 0.0 reduce-scatter.7.cloned.1.call-start
  177.6 51.2 %reduce-scatter.5.cloned.1.call-done = f32[128,2560]{1,0:T(8,128)} async-done(((f32[512,2560]{1,0:T(8,128)}), f32[128,2560]{1,0:T(8,128)}) %reduce-scatter.5.cloned.1.call-update) | async-done | bytes 1310736 | tf_op jit(solution)/shard_map/reduce_scatter | solution.py:59
  228.8 2.8 copy.15
  231.6 0.0 reduce-scatter.7.cloned.1.call-update
  231.6 0.6 dynamic_slice.3
  232.2 4.8 %convolution_convert_fusion = bf16[512,2560]{1,0:T(8,128)(2,1)} fusion(bf16[512,512]{0,1:T(8,128)(2,1)S(1)} %fusion.7, bf16[512,2560]{1,0:T(8,128)(2,1)} %all-gather.6.cloned.1.call-done), kind=kOutput, calls=%fused_computation.2 | convolution fusion | flops 1343488000 | bytes 5767168 | tf_op jit(solution)/shard_map/dot_general | solution.py:56
  236.9 60.3 %reduce-scatter.7.cloned.1.call-done = f32[320,128]{1,0:T(8,128)} async-done(((f32[2560,128]{1,0:T(8,128)}), f32[320,128]{1,0:T(8,128)}) %reduce-scatter.7.cloned.1.call-update) | async-done | bytes 163856
  297.2 1.0 copy.16
  298.2 0.8 copy.14
  (2 shorter events, 0.0 us)
Async XLA Ops:
  7.2 30.7 %copy-start = (bf16[512,2560]{1,0:T(8,128)(2,1)S(1)}, bf16[512,2560]{1,0:T(8,128)(2,1)}, u32[]{:S(2)}) copy-start(bf16[512,2560]{1,0:T(8,128)(2,1)} %param.10) | copy-start | bytes 7864324
  7.2 30.7 %all-gather.6.cloned.1.call-start = ((), (), s32[]{:S(2)}) async-start(), calls=%async_computation.3 | async-start | bytes 3276800 | tf_op jit(solution)/shard_map/all_gather | solution.py:27
  7.9 73.4 %all-gather.4.cloned.1.call-start = ((), (), s32[]{:S(2)}) async-start(), calls=%async_computation.2 | async-start | bytes 6881280 | tf_op jit(solution)/shard_map/all_gather | solution.py:26
  8.7 8.3 %copy-start.2 = (bf16[128]{0:T(256)(128)(2,1)S(1)}, bf16[128]{0:T(256)(128)(2,1)}, u32[]{:S(2)}) copy-start(bf16[128]{0:T(256)(128)(2,1)} %param.11) | copy-start | bytes 772
  8.7 14.4 %copy-start.1 = (f32[512,42]{0,1:T(8,128)S(1)}, f32[512,42]{0,1:T(8,128)}, u32[]{:S(2)}) copy-start(f32[512,42]{0,1:T(8,128)} %param.9) | copy-start | bytes 258052
  8.7 220.1 %reduce-scatter.5.cloned.1.call-start = ((), (), s32[]{:S(2)}) async-start(), calls=%async_computation.4 | async-start | bytes 6553600 | tf_op jit(solution)/shard_map/reduce_scatter | solution.py:59
  177.6 119.7 %reduce-scatter.7.cloned.1.call-start = ((), (), s32[]{:S(2)}) async-start(), calls=%async_computation.5 | async-start | bytes 1474560
Sparse Core Ops, SparseCore 0:
  9.5 28.2 all-gather.5
  39.4 41.8 all-gather.3
  177.7 51.0 reduce-scatter.4
  232.0 65.1 reduce-scatter.6
where the time goes:
time: 306 us
  waiting for transfers between devices  161 us (53%)
  blocking collectives  86.3 us (28%)
  matrix products  21.1 us (7%)
  between operations  13.8 us (5%)
  local copies, waits for them, and re-layouts  13.4 us (4%)
  other arithmetic  9.94 us (3%)
    unnamed x5, waiting for transfers between devices  61.7 us
    reduce_scatter x1, waiting for transfers between devices, local(): lax.psum_scatter(jnp.dot(logit_grad, student_weight, preferred_element_ty...  51.2 us
    psum x1, blocking collectives, local(): lax.psum((jnp.sum(teacher_exp, axis=1), jnp.sum(teacher_exp * (teacher_lo...  41.1 us
    pmax x1, blocking collectives, local(): lax.pmax((teacher_local, student_local), ('vocab', 'dp'))  39.2 us
    all_gather x1, waiting for transfers between devices, local(): lax.all_gather(teacher_hidden, 'dp', axis=0, tiled=True)  39.2 us
    unnamed x10, local copies, waits for them, and re-layouts  12.9 us
    dot_general x2, matrix products, contract_last(): lax.dot_general(left_rows, right_rows, (((1,), (1,)), ((), ())), preferre...  12.5 us
    all_gather x1, waiting for transfers between devices, local(): lax.all_gather(student_hidden, 'dp', axis=0, tiled=True)  8.66 us
  transfers between devices with their start and end apart: 4, of which 4 were waited for; matrix products, arithmetic and copies ran while one was open for 8% of the time, Pallas kernels for 0%

commit v1 on v0

--- a/solution.py
+++ b/solution.py
@@ -23,7 +23,9 @@
 ):
     tok_rows = teacher_hidden.shape[0]
     teacher_all, student_all, scale_all = (
-        lax.all_gather(teacher_hidden, "dp", axis=0, tiled=True),
+        jnp.concatenate(
+            lax.all_to_all(jnp.stack([teacher_hidden] * lax.axis_size("dp")), "dp", 0, 0), axis=0
+        ),
         lax.all_gather(student_hidden, "dp", axis=0, tiled=True),
         lax.all_gather(loss_scale, "dp", axis=0, tiled=True),
     )

time: 306 us -> 340 us (1.11)
  blocking collectives: 86.3 us -> 159 us
  waiting for transfers between devices: 161 us -> 112 us
  starting transfers between devices: 0.16 us -> 5.34 us
  local copies, waits for them, and re-layouts: 13.4 us -> 17.7 us
    all_gather x1, blocking collectives: 6.02 us -> 77.7 us  [local(): lax.all_gather(loss_scale, 'dp', axis=0, tiled=True)]
    all_gather x1 -> x0, waiting for transfers between devices: 39.2 us -> none  [local(): lax.all_gather(teacher_hidden, 'dp', axis=0, tiled=True)]
    all_gather x1, waiting for transfers between devices: 8.66 us -> 0.01 us  [local(): lax.all_gather(student_hidden, 'dp', axis=0, tiled=True)]
    all_to_all x0 -> x1, starting transfers between devices: none -> 5.22 us  [local(): lax.all_to_all(jnp.stack([teacher_hidden] * lax.axis_size('dp')), 'dp', 0...]
    another operation x0 -> x1, local copies, waits for them, and re-layouts: none -> 4.19 us  [local(): jnp.stack([teacher_hidden] * lax.axis_size('dp'))]
    unnamed x5 -> x4, waiting for transfers between devices: 61.7 us -> 61 us
  transfers between devices with their start and end apart: 4 -> 4, of which waited for: 4 -> 2; matrix products, arithmetic and copies ran while one was open for 8% -> 8% of each run, Pallas kernels for 0% -> 0%
where the time goes in v1:
time: 340 us; the launch traced here: 339 us
  blocking collectives  159 us (47%)
  waiting for transfers between devices  112 us (33%)
  matrix products  21.1 us (6%)
  local copies, waits for them, and re-layouts  17.7 us (5%)
  between operations  13.8 us (4%)
  other arithmetic  9.84 us (3%)
  starting transfers between devices  5.34 us (2%)
    all_gather x1, blocking collectives, local(): lax.all_gather(loss_scale, 'dp', axis=0, tiled=True)  77.7 us
    unnamed x4, waiting for transfers between devices  61 us
    reduce_scatter x1, waiting for transfers between devices, local(): lax.psum_scatter(jnp.dot(logit_grad, student_weight, preferred_element_ty...  51.2 us
    psum x1, blocking collectives, local(): lax.psum((jnp.sum(teacher_exp, axis=1), jnp.sum(teacher_exp * (teacher_lo...  41 us
    pmax x1, blocking collectives, local(): lax.pmax((teacher_local, student_local), ('vocab', 'dp'))  40.2 us
    unnamed x10, local copies, waits for them, and re-layouts  12.9 us
    dot_general x2, matrix products, contract_last(): lax.dot_general(left_rows, right_rows, (((1,), (1,)), ((), ())), preferre...  12.5 us
  transfers between devices with their start and end apart: 4, of which 2 were waited for; matrix products, arithmetic and copies ran while one was open for 8% of the time, Pallas kernels for 0%

profile of v1, /device:TPU:0, one launch (start us, length us, event | category | flops | bytes accessed | tf_op | source)
XLA Modules:
  0.0 339.1 jit_solution(4366638004036172114)
XLA Ops:
  7.2 0.0 copy-start
  7.2 0.0 all-gather.3.cloned.1.call-start
  7.2 0.7 all-gather.3.cloned.1.call-update
  7.9 4.2 %stack.2 = bf16[4,128,5376]{2,1,0:T(8,128)(2,1)} broadcast(bf16[128,5376]{1,0:T(8,128)(2,1)} %param.6), dimensions={1,2} | broadcast | bytes 6881280 | tf_op jit(solution)/shard_map/stack | solution.py:27
  12.1 0.0 copy-start.2
  12.1 5.2 %all-to-all-start = ((bf16[4,128,5376]{2,1,0:T(8,128)(2,1)}), bf16[4,128,5376]{2,1,0:T(8,128)(2,1)}, u32[]{:S(2)}, u32[]{:S(2)}) async-start(bf16[4,128,5376]{2,1,0:T(8,128)(2,1)} %stack.2), calls=%async_computation | async-start | bytes 11010048 | tf_op jit(solution)/shard_map/all_to_all | solution.py:27
  17.3 0.0 reduce-scatter.5.cloned.1.call-start
  17.4 0.0 copy-done.2
  17.4 77.7 %all-gather = bf16[4,1,128]{2,1,0:T(2,128)(2,1)S(1)} all-gather(bf16[1,1,128]{2,1,0:T(2,128)(2,1)S(1)} %bitcast.42), channel_id=1, replica_groups=mesh['vocab'=8,'dp'=4] {'dp'}, dimensions={0}, use_global_device_ids=true | all-gather | bytes 1280 | tf_op jit(solution)/shard_map/all_gather | solution.py:30
  95.1 0.0 copy-start.1
  95.1 8.4 %copy.13 = bf16[512,5376]{0,1:T(8,128)(2,1)} copy(bf16[512,5376]{1,0:T(8,128)(2,1)} %param.8) | data formatting | bytes 11010048 | tf_op args[2]
  103.5 0.0 copy-done.1
  103.5 6.0 %fusion = bf16[512,5376]{0,1:T(8,128)(2,1)} fusion(bf16[512,5376]{0,1:T(8,128)(2,1)} %copy.13, f32[512,42]{0,1:T(8,128)S(1)} %copy-done.1), kind=kLoop, calls=%fused_computation.1 | loop fusion | flops 8257536 | bytes 11096064 | tf_op jit(solution)/shard_map/convert_element_type | solution.py:12
  109.5 0.0 all-gather.3.cloned.1.call-done
  109.5 0.0 copy-done
  109.5 4.3 %fusion.9 = (f32[512]{0:T(512)S(1)}, f32[512,512]{0,1:T(8,128)}) fusion(bf16[512,2560]{1,0:T(8,128)(2,1)} %all-gather.3.cloned.1.call-done, bf16[512,2560]{1,0:T(8,128)(2,1)S(1)} %copy-done), kind=kOutput, calls=%fused_computation.18 | convolution fusion | flops 1342438912 | bytes 6293504 | tf_op jit(solution)/shard_map/dot_general | solution.py:16
  113.8 0.0 all-to-all-done
  113.8 8.3 %fusion.10 = (f32[512]{0:T(512)S(1)}, f32[512,512]{1,0:T(8,128)}) fusion(bf16[512,5376]{0,1:T(8,128)(2,1)} %fusion, bf16[512,5376]{1,0:T(8,128)(2,1)} %bitcast.1), kind=kOutput, calls=%fused_computation.19 | convolution fusion | flops 2818833920 | bytes 12060672 | tf_op jit(solution)/shard_map/dot_general | solution.py:16
  122.1 40.2 %all-reduce.1 = (f32[512]{0:T(512)S(1)}, f32[512]{0:T(512)S(1)}) all-reduce(f32[512]{0:T(512)S(1)} %get-tuple-element.23, f32[512]{0:T(512)S(1)} %get-tuple-element.25), channel_id=1, replica_groups=mesh['vocab'=8,'dp'=4] {'vocab','dp'}, use_global_device_ids=true, to_apply=%region_7.0 | all-reduce | flops 1024 | bytes 8192 | tf_op jit(solution)/shard_map/pmax | solution.py:37
  162.3 1.9 fusion.3
  164.2 41.0 %all-reduce = (f32[512]{0:T(512)S(1)}, f32[512]{0:T(512)S(1)}, f32[512]{0:T(512)S(1)}) all-reduce(f32[512]{0:T(512)S(1)} %get-tuple-element.14, f32[512]{0:T(512)S(1)} %get-tuple-element.13, f32[512]{0:T(512)S(1)} %get-tuple-element.12), channel_id=1, replica_groups=mesh['vocab'=8,'dp'=4] {'vocab','dp'}, use_global_device_ids=true, to_apply=%region_9.0 | all-reduce | flops 1536 | bytes 12288 | tf_op jit(solution)/shard_map/psum | solution.py:40
  205.3 1.8 fusion.7
  207.1 3.9 %fusion.11 = f32[512,2560]{1,0:T(8,128)} fusion(bf16[512,512]{0,1:T(8,128)(2,1)S(1)} %fusion.7, bf16[512,2560]{1,0:T(8,128)(2,1)S(1)} %copy-done), kind=kOutput, calls=%fused_computation.20 | convolution fusion | flops 1342177280 | bytes 8388608 | tf_op jit(solution)/shard_map/dot_general | solution.py:62
  211.0 0.0 reduce-scatter.5.cloned.1.call-update
  211.0 0.0 reduce-scatter.7.cloned.1.call-start
  211.1 51.2 %reduce-scatter.5.cloned.1.call-done = f32[128,2560]{1,0:T(8,128)} async-done(((f32[512,2560]{1,0:T(8,128)}), f32[128,2560]{1,0:T(8,128)}) %reduce-scatter.5.cloned.1.call-update) | async-done | bytes 1310736 | tf_op jit(solution)/shard_map/reduce_scatter | solution.py:61
  262.3 2.8 copy.15
  265.1 0.0 reduce-scatter.7.cloned.1.call-update
  265.1 0.6 dynamic_slice.3
  265.7 4.8 %convolution_convert_fusion = bf16[512,2560]{1,0:T(8,128)(2,1)} fusion(bf16[512,512]{0,1:T(8,128)(2,1)S(1)} %fusion.7, bf16[512,2560]{1,0:T(8,128)(2,1)} %all-gather.3.cloned.1.call-done), kind=kOutput, calls=%fused_computation.2 | convolution fusion | flops 1343488000 | bytes 5767168 | tf_op jit(solution)/shard_map/dot_general | solution.py:58
  270.5 60.3 %reduce-scatter.7.cloned.1.call-done = f32[320,128]{1,0:T(8,128)} async-done(((f32[2560,128]{1,0:T(8,128)}), f32[320,128]{1,0:T(8,128)}) %reduce-scatter.7.cloned.1.call-update) | async-done | bytes 163856
  330.7 1.0 copy.16
  331.8 0.8 copy.14
  (2 shorter events, 0.0 us)
Async XLA Ops:
  7.2 102.4 %copy-start = (bf16[512,2560]{1,0:T(8,128)(2,1)S(1)}, bf16[512,2560]{1,0:T(8,128)(2,1)}, u32[]{:S(2)}) copy-start(bf16[512,2560]{1,0:T(8,128)(2,1)} %param.10) | copy-start | bytes 7864324
  7.2 102.4 %all-gather.3.cloned.1.call-start = ((), (), s32[]{:S(2)}) async-start(), calls=%async_computation.3 | async-start | bytes 3276800 | tf_op jit(solution)/shard_map/all_gather | solution.py:29
  12.1 5.3 %copy-start.2 = (bf16[128]{0:T(256)(128)(2,1)S(1)}, bf16[128]{0:T(256)(128)(2,1)}, u32[]{:S(2)}) copy-start(bf16[128]{0:T(256)(128)(2,1)} %param.11) | copy-start | bytes 772
  12.1 101.7 %all-to-all-start = ((bf16[4,128,5376]{2,1,0:T(8,128)(2,1)}), bf16[4,128,5376]{2,1,0:T(8,128)(2,1)}, u32[]{:S(2)}, u32[]{:S(2)}) async-start(bf16[4,128,5376]{2,1,0:T(8,128)(2,1)} %stack.2), calls=%async_computation | async-start | bytes 11010048 | tf_op jit(solution)/shard_map/all_to_all | solution.py:27
  17.3 245.0 %reduce-scatter.5.cloned.1.call-start = ((), (), s32[]{:S(2)}) async-start(), calls=%async_computation.4 | async-start | bytes 6553600 | tf_op jit(solution)/shard_map/reduce_scatter | solution.py:61
  95.1 8.4 %copy-start.1 = (f32[512,42]{0,1:T(8,128)S(1)}, f32[512,42]{0,1:T(8,128)}, u32[]{:S(2)}) copy-start(f32[512,42]{0,1:T(8,128)} %param.9) | copy-start | bytes 258052
  211.0 119.7 %reduce-scatter.7.cloned.1.call-start = ((), (), s32[]{:S(2)}) async-start(), calls=%async_computation.5 | async-start | bytes 1474560
Sparse Core Ops, SparseCore 0:
  9.5 42.3 all-gather.2
  211.1 51.1 reduce-scatter.4
  265.7 64.9 reduce-scatter.6
